TPU v7x, 32 devices: a whole 2x2x4 slice. The times are simulated.
32 devices in a mesh: group: 2 (over x), tp: 16 (over z, y, core), pool: 1.
Axes of the slice: x: 2, y: 2, z: 4, core: 2. Of those that a mesh axis runs over, the one named last changes fastest.
Arguments:
- prompt_x: bfloat16 [2048, 8192], P(('group', 'pool'), 'tp'), parts along dimension 0, may hold values from -6 to 6
- decode_x: bfloat16 [4, 32, 8192], P(None, ('group', 'pool'), 'tp'), parts along dimension 1, may hold values from -240 to 240
- w_query: bfloat16 [8192, 8192], P(None, 'tp'), may hold values from -0.0625 to 0.0625
- w_keyval: bfloat16 [8192, 2048], P('tp'), may hold values from -0.0625 to 0.0625
- w_out: bfloat16 [8192, 8192], P('tp'), may hold values from -0.0625 to 0.0625
- prompt_blocks: int32 [32], P('group'), parts along dimension 0, may hold values from 1 to 32, 64 in all
- prompt_row: int32 [32], P('group'), parts along dimension 0, may hold values from 0 to 15, each once
Outputs:
- decode_out: bfloat16 [4, 32, 8192], P(None, ('group', 'pool'), 'tp'), parts along dimension 1
There are 2 independent parts, one for each index of `group`. A program takes and returns all parts, laid end to end along the dimension named above; an argument that names none is the same for every part. Nothing has to cross between parts.
Inputs may be any that keep to these rules, and one draw needn't show every extreme that they name: `prompt_blocks`: each prompt has at least one block, the prompts fill the span exactly, and one prompt has exactly 32 blocks. `prompt_row`: every decode row continues exactly one prompt.
All inputs are finite; a program needn't handle non-finite values. Where the computation divides by a largest or mean magnitude, that divisor is 1e-20 or more.
Results may differ from a plain program's by a relative error of at most 0.018.
Values may be sent and summed in bfloat16 or wider, within the bound.
No kernel may reach another device: no remote copies, remote signals or barrier semaphores. Data moves between devices by JAX's collectives and lax.ppermute only.
A program may use at most 128 MiB of HBM per device.

v0:
```python
import math

import jax
import jax.numpy as jnp
import numpy as np
from jax import lax
from jax.sharding import PartitionSpec as P

KVH = 8
HD = 128
BLK = 16


def block_rows(prompt_blocks, prompt_row, total_blocks):
    block_ends = jnp.cumsum(prompt_blocks)
    positions = jnp.arange(total_blocks, dtype=jnp.int32)
    owner_seq = jnp.sum((block_ends[None, :] <= positions[:, None]).astype(jnp.int32), axis=1)
    seq_match = owner_seq[:, None] == jnp.arange(prompt_row.shape[0], dtype=jnp.int32)[None, :]
    return jnp.sum(jnp.where(seq_match, prompt_row[None, :], 0), axis=1)


def attend(queries, cache_vals, cache_scale, slot_row, fresh_keyval, row_ids):
    head_dim = queries.shape[-1]
    inverse_root = 1.0 / math.sqrt(head_dim)
    query_f32 = queries.astype(jnp.float32)
    scale_f32 = cache_scale.astype(jnp.float32)
    cache_keys = cache_vals[:, :, :head_dim].astype(jnp.float32) * scale_f32[:, 0][:, None, None]
    cache_values = cache_vals[:, :, head_dim:].astype(jnp.float32) * scale_f32[:, 1][:, None, None]
    cache_score = jnp.einsum("srgd,nkd->srgnk", query_f32, cache_keys) * inverse_root
    visible = slot_row[None, :] == row_ids[:, None]
    cache_score = jnp.where(visible[None, :, None, :, None], cache_score, -jnp.inf)
    fresh_f32 = fresh_keyval.astype(jnp.float32)
    fresh_score = jnp.einsum("srgd,trd->srgt", query_f32, fresh_f32[:, :, :head_dim]) * inverse_root
    step_index = jnp.arange(queries.shape[0], dtype=jnp.int32)
    causal = step_index[:, None] >= step_index[None, :]
    fresh_score = jnp.where(causal[:, None, None, :], fresh_score, -jnp.inf)
    top_score = jnp.maximum(jnp.max(cache_score, axis=(3, 4)), jnp.max(fresh_score, axis=3))
    cache_weight = jnp.exp(cache_score - top_score[..., None, None])
    fresh_weight = jnp.exp(fresh_score - top_score[..., None])
    denominator = jnp.sum(cache_weight, axis=(3, 4)) + jnp.sum(fresh_weight, axis=3)
    weighted = jnp.einsum("srgnk,nkd->srgd", cache_weight, cache_values)
    weighted = weighted + jnp.einsum("srgt,trd->srgd", fresh_weight, fresh_f32[:, :, head_dim:])
    return weighted / denominator[..., None]


def on_device(prompt_x, decode_x, w_query, w_keyval, w_out, prompt_blocks, prompt_row):
    tp_count = lax.axis_size("tp")
    pool_count = lax.axis_size("pool")
    tp_index = lax.axis_index("tp")
    pool_index = lax.axis_index("pool")
    half_tokens = prompt_x.shape[0]
    tokens_here = half_tokens // tp_count
    blocks_here = tokens_here // BLK
    half_blocks = half_tokens // BLK
    total_blocks = half_blocks * pool_count
    keyval = lax.psum_scatter(
        jnp.dot(prompt_x, w_keyval, preferred_element_type=jnp.float32),
        "tp",
        scatter_dimension=0,
        tiled=True,
    )
    blocked = keyval.reshape(blocks_here, BLK, KVH, 2, HD)
    scales = (jnp.max(jnp.abs(blocked), axis=(1, 4)) + 1e-06).astype(jnp.bfloat16)
    stored = (blocked / scales.astype(jnp.float32)[:, None, :, :, None]).astype(jnp.bfloat16)
    stored = stored.reshape(blocks_here, BLK, KVH, 2 * HD)
    slot_row_all = block_rows(prompt_blocks, prompt_row, total_blocks)
    row_half = decode_x.shape[1]
    owner_half = slot_row_all // row_half
    first_block = pool_index * half_blocks + tp_index * blocks_here
    mine_owner = lax.dynamic_slice_in_dim(owner_half, first_block, blocks_here, 0)
    dest_head = np.arange(tp_count) * KVH // tp_count
    by_head = stored.transpose(2, 0, 1, 3)[dest_head]
    scale_head = scales.transpose(1, 0, 2)[dest_head]
    to_half = mine_owner[None, :] == jnp.arange(pool_count, dtype=jnp.int32)[:, None]
    zero_value = jnp.zeros((), jnp.bfloat16)
    send_vals = jnp.where(to_half[None, :, :, None, None], by_head[:, None], zero_value)
    send_scale = jnp.where(to_half[None, :, :, None], scale_head[:, None], zero_value)
    got_vals, got_scale = (
        lax.all_to_all(
            lax.all_to_all(send_vals, "tp", split_axis=0, concat_axis=0, tiled=True),
            "pool",
            split_axis=1,
            concat_axis=1,
            tiled=True,
        ),
        lax.all_to_all(
            lax.all_to_all(send_scale, "tp", split_axis=0, concat_axis=0, tiled=True),
            "pool",
            split_axis=1,
            concat_axis=1,
            tiled=True,
        ),
    )
    got_vals = got_vals.reshape(total_blocks, BLK, 2 * HD)
    got_scale = got_scale.reshape(total_blocks, 2)
    slot_row = (
        slot_row_all.reshape(pool_count, tp_count, blocks_here)
        .transpose(1, 0, 2)
        .reshape(total_blocks)
    )
    gathered = lax.all_gather(decode_x, "tp", axis=2, tiled=True)
    step_count, row_count, model_width = gathered.shape
    heads_here = w_query.shape[1] // HD
    queries = jnp.einsum("srd,de->sre", gathered, w_query, preferred_element_type=jnp.float32)
    queries = queries.astype(jnp.bfloat16).reshape(step_count, row_count, heads_here, HD)
    partial_new = jnp.einsum("srd,de->sre", decode_x, w_keyval, preferred_element_type=jnp.float32)
    summed_new = lax.psum(partial_new, "tp")
    fresh_keyval = summed_new.astype(jnp.bfloat16).reshape(step_count, row_count, KVH, 2 * HD)
    my_head = tp_index * KVH // tp_count
    fresh_keyval = lax.dynamic_index_in_dim(fresh_keyval, my_head, 2, keepdims=False)
    row_ids = pool_index * row_count + jnp.arange(row_count, dtype=jnp.int32)
    weighted = attend(queries, got_vals, got_scale, slot_row, fresh_keyval, row_ids)
    attended = weighted.reshape(step_count, row_count, heads_here * HD).astype(jnp.bfloat16)
    out_term = jnp.einsum("sre,ed->srd", attended, w_out, preferred_element_type=jnp.float32)
    return lax.psum_scatter(out_term, "tp", scatter_dimension=2, tiled=True).astype(jnp.bfloat16)


def solution(mesh):
    placed = (
        P(("group", "pool"), "tp"),
        P(None, ("group", "pool"), "tp"),
        P(None, "tp"),
        P("tp", None),
        P("tp", None),
        P("group"),
        P("group"),
    )
    return jax.shard_map(
        on_device,
        mesh=mesh,
        in_specs=placed,
        out_specs=P(None, ("group", "pool"), "tp"),
        check_vma=False,
    )
```

profile of v0, /device:TPU:0, one launch (start us, length us, event | category | flops | bytes accessed | tf_op | source)
XLA Modules:
  0.0 254.8 jit_solution(7903377930404320485)
XLA Ops:
  6.5 0.0 copy-start
  6.5 0.0 reduce-scatter.3.cloned.1.call-start
  6.5 1.6 copy-done
  8.1 6.8 %fusion.50 = f32[1024,2048]{1,0:T(8,128)} fusion(bf16[1024,512]{1,0:T(8,128)(2,1)} %param.10, bf16[512,2048]{1,0:T(8,128)(2,1)S(1)} %copy-done), kind=kOutput, calls=%fused_computation.76 | convolution fusion | flops 2147483648 | bytes 11534336 | tf_op jit(solution)/shard_map/dot_general | solution.py:57
  14.9 0.0 copy-start.2
  14.9 0.0 reduce-scatter.3.cloned.1.call-update
  14.9 0.0 all-gather.2.cloned.1.call-start
  15.0 0.7 all-gather.2.cloned.1.call-update
  15.7 0.0 copy-start.3
  15.7 0.0 copy-done.2
  15.8 0.0 copy-start.5
  15.8 0.5 fusion.4
  16.3 74.8 %all-reduce.1 = bf16[4,16,2048]{2,1,0:T(8,128)(2,1)S(1)} all-reduce(f32[4,16,2048]{2,1,0:T(8,128)S(1)} %fusion.4), channel_id=1, replica_groups=mesh['group'=2,'tp'=16,'pool'=1] {'tp'}, use_global_device_ids=true, to_apply=%region_6.7 | all-reduce | flops 131072 | bytes 786432 | tf_op jit(solution)/shard_map/psum | solution.py:107
  91.0 0.1 copy.124
  91.1 0.1 constant_dynamic-slice_fusion
  91.2 0.0 copy-done.3
  91.2 0.1 copy.90
  91.3 0.1 reduce
  91.5 0.1 convert_reduce_fusion
  91.6 0.0 copy-done.5
  91.6 0.1 select_reduce_fusion
  91.7 0.1 dynamic-slice_compare_fusion
  91.8 0.0 copy-done.4
  91.8 32.1 %reduce-scatter.3.cloned.1.call-done = f32[64,2048]{1,0:T(8,128)} async-done(((f32[1024,2048]{1,0:T(8,128)}), f32[64,2048]{1,0:T(8,128)}) %reduce-scatter.3.cloned.1.call-update) | async-done | bytes 524304 | tf_op jit(solution)/shard_map/reduce_scatter | solution.py:56
  123.8 1.9 abs.6
  125.8 1.5 abs.7
  127.3 0.2 reduce_max.27
  127.5 0.1 copy.91
  127.6 0.1 copy.92
  127.7 0.1 div.45
  127.9 0.0 copy-done.1
  127.9 0.2 copy.123
  128.0 0.1 copy.96
  128.1 0.2 fusion.36
  128.3 0.6 gather_fusion
  128.9 0.6 gather_fusion.1
  129.5 0.1 copy.97
  129.6 0.1 bitcast_select_fusion.1
  129.7 0.7 copy.98
  130.4 4.3 %all-to-all-start.1 = ((bf16[16,1,4,2]{2,3,1,0:T(2,128)(2,1)}), bf16[16,1,4,2]{2,3,1,0:T(2,128)(2,1)S(1)}, u32[]{:S(2)}, u32[]{:S(2)}) async-start(bf16[16,1,4,2]{2,3,1,0:T(2,128)(2,1)} %copy.98), calls=%async_computation.2 | async-start | bytes 16384 | tf_op jit(solution)/shard_map/all_to_all | solution.py:87
  134.7 0.9 fusion.26
  135.6 5.5 %all-to-all-done.1 = bf16[16,1,4,2]{2,3,1,0:T(2,128)(2,1)S(1)} async-done(((bf16[16,1,4,2]{2,3,1,0:T(2,128)(2,1)}), bf16[16,1,4,2]{2,3,1,0:T(2,128)(2,1)S(1)}, u32[]{:S(2)}, u32[]{:S(2)}) %all-to-all-start.1) | async-done | bytes 288 | tf_op jit(solution)/shard_map/all_to_all | solution.py:87
  141.1 3.6 %all-to-all-start = ((bf16[16,1,4,16,256]{4,3,2,1,0:T(8,128)(2,1)}), bf16[16,1,4,16,256]{4,3,2,1,0:T(8,128)(2,1)S(1)}, u32[]{:S(2)}, u32[]{:S(2)}) async-start(bf16[16,1,4,16,256]{4,3,2,1,0:T(8,128)(2,1)} %fusion.26), calls=%async_computation.1 | async-start | bytes 1048576 | tf_op jit(solution)/shard_map/all_to_all | solution.py:80
  144.7 0.0 reduce-scatter.5.cloned.1.call-start
  144.8 20.9 %all-gather.2.cloned.1.call-done = bf16[4,16,8192]{2,1,0:T(8,128)(2,1)} async-done(((bf16[4,16,512]{2,1,0:T(8,128)(2,1)}), bf16[4,16,8192]{2,1,0:T(8,128)(2,1)}) %all-gather.2.cloned.1.call-update) | async-done | bytes 1048592 | tf_op jit(solution)/shard_map/all_gather | solution.py:101
  165.7 5.3 %fusion.15 = bf16[4,16,512]{2,1,0:T(8,128)(2,1)S(1)} fusion(bf16[4,16,8192]{2,1,0:T(8,128)(2,1)} %all-gather.2.cloned.1.call-done, bf16[8192,512]{1,0:T(8,128)(2,1)} %param.12), kind=kOutput, calls=%fused_computation.20 | convolution fusion | flops 536903680 | bytes 9502720 | tf_op jit(solution)/shard_map/srd,de->sre/dot_general | solution.py:104
  171.0 0.7 fusion.49
  171.7 0.1 copy.104
  171.8 0.1 copy.99
  171.9 0.1 copy.100
  172.0 0.1 reshape.136
  172.1 0.0 all-to-all-done
  172.1 0.1 fusion.48
  172.2 1.9 fusion.6
  174.1 0.1 copy.106
  174.2 0.2 fusion.38
  174.5 0.1 fusion.37
  174.6 2.2 fusion.7
  176.8 0.1 copy.109
  176.9 2.3 fusion.18
  179.2 6.3 %fusion = f32[4,16,8192]{2,1,0:T(8,128)} fusion(bf16[512,8192]{1,0:T(8,128)(2,1)} %param.14, bf16[4,4,2,8,128]{4,3,2,1,0:T(8,128)(2,1)S(1)} %fusion.18), kind=kOutput, calls=%fused_computation.2 | convolution fusion | flops 536870912 | bytes 10551296 | tf_op jit(solution)/shard_map/sre,ed->srd/dot_general | solution.py:114
  185.6 0.0 reduce-scatter.5.cloned.1.call-update
  185.6 61.2 %reduce-scatter.5.cloned.1.call-done = f32[4,16,512]{2,1,0:T(8,128)} async-done(((f32[4,16,8192]{2,1,0:T(8,128)}), f32[4,16,512]{2,1,0:T(8,128)}) %reduce-scatter.5.cloned.1.call-update) | async-done | bytes 131088 | tf_op jit(solution)/shard_map/reduce_scatter | solution.py:115
  246.8 1.5 convert_element_type.67
  (14 shorter events, 0.2 us)
Async XLA Ops:
  6.5 1.6 copy-start
  6.5 117.3 %reduce-scatter.3.cloned.1.call-start = ((), (), s32[]{:S(2)}) async-start(), calls=%async_computation.5 | async-start | bytes 8912896 | tf_op jit(solution)/shard_map/reduce_scatter | solution.py:56
  14.9 0.8 copy-start.2
  14.9 150.7 %all-gather.2.cloned.1.call-start = ((), (), s32[]{:S(2)}) async-start(), calls=%async_computation.4 | async-start | bytes 1114112 | tf_op jit(solution)/shard_map/all_gather | solution.py:101
  15.7 75.5 %copy-start.3 = (s32[16]{0:T(128)S(1)}, s32[16]{0:T(128)}, u32[]{:S(2)}) copy-start(s32[16]{0:T(128)} %param.15) | copy-start | bytes 196
  15.8 75.8 %copy-start.5 = (s32[16]{0:T(128)S(1)}, s32[16]{0:T(128)}, u32[]{:S(2)}) copy-start(s32[16]{0:T(128)} %param.16) | copy-start | bytes 196
  15.8 76.0 %copy-start.4 = (s32[16]{0:T(128)S(1)}, s32[16]{0:T(128)}, u32[]{:S(2)}) copy-start(s32[16]{0:T(128)} %constant.66) | copy-start | bytes 196
  123.8 4.0 %copy-start.1 = (f32[64,2048]{1,0:T(8,128)S(1)}, f32[64,2048]{1,0:T(8,128)}, u32[]{:S(2)}) copy-start(f32[64,2048]{1,0:T(8,128)} %reduce-scatter.3.cloned.1.call-done) | copy-start | bytes 1572868
  130.4 10.8 %all-to-all-start.1 = ((bf16[16,1,4,2]{2,3,1,0:T(2,128)(2,1)}), bf16[16,1,4,2]{2,3,1,0:T(2,128)(2,1)S(1)}, u32[]{:S(2)}, u32[]{:S(2)}) async-start(bf16[16,1,4,2]{2,3,1,0:T(2,128)(2,1)} %copy.98), calls=%async_computation.2 | async-start | bytes 16384 | tf_op jit(solution)/shard_map/all_to_all | solution.py:87
  141.1 31.0 %all-to-all-start = ((bf16[16,1,4,16,256]{4,3,2,1,0:T(8,128)(2,1)}), bf16[16,1,4,16,256]{4,3,2,1,0:T(8,128)(2,1)S(1)}, u32[]{:S(2)}, u32[]{:S(2)}) async-start(bf16[16,1,4,16,256]{4,3,2,1,0:T(8,128)(2,1)} %fusion.26), calls=%async_computation.1 | async-start | bytes 1048576 | tf_op jit(solution)/shard_map/all_to_all | solution.py:80
  144.7 102.1 %reduce-scatter.5.cloned.1.call-start = ((), (), s32[]{:S(2)}) async-start(), calls=%async_computation.6 | async-start | bytes 2228224 | tf_op jit(solution)/shard_map/reduce_scatter | solution.py:115
Sparse Core Ops, SparseCore 0:
  15.1 108.7 reduce-scatter.2
  126.0 39.6 all-gather.1
  185.7 61.0 reduce-scatter.4
where the time goes:
time: 255 us
  waiting for transfers between devices  120 us (47%)
  blocking collectives  74.8 us (29%)
  matrix products  24 us (9%)
  between operations  13.3 us (5%)
  starting transfers between devices  7.99 us (3%)
  other arithmetic  7.65 us (3%)
  local copies, waits for them, and re-layouts  6.69 us (3%)
    psum x1, blocking collectives, on_device(): summed_new = lax.psum(partial_new, 'tp')  74.8 us
    reduce_scatter x1, waiting for transfers between devices, on_device(): lax.psum_scatter(out_term, 'tp', scatter_dimension=2, tiled=True)  61.2 us
    reduce_scatter x1, waiting for transfers between devices, on_device(): lax.psum_scatter(jnp.dot(prompt_x, w_keyval, preferred_element_type=jnp.f...  32.1 us
    all_gather x1, waiting for transfers between devices, on_device(): gathered = lax.all_gather(decode_x, 'tp', axis=2, tiled=True)  20.9 us
    dot_general x1, matrix products, on_device(): jnp.dot(prompt_x, w_keyval, preferred_element_type=jnp.float32)  6.79 us
    dot_general x1, matrix products, on_device(): jnp.einsum('sre,ed->srd', attended, w_out, preferred_element_type=jnp.flo...  6.33 us
    all_to_all x1, waiting for transfers between devices, on_device(): lax.all_to_all(send_scale, 'tp', split_axis=0, concat_axis=0, tiled=True)  5.52 us
    dot_general x1, matrix products, on_device(): jnp.einsum('srd,de->sre', gathered, w_query, preferred_element_type=jnp.f...  5.27 us
  transfers between devices with their start and end apart: 5, of which 4 were waited for; matrix products, arithmetic and copies ran while one was open for 6% of the time, Pallas kernels for 0%

commit v1 on v0

--- a/solution.py
+++ b/solution.py
@@ -4,11 +4,16 @@
 import jax.numpy as jnp
 import numpy as np
 from jax import lax
+from jax.experimental import pallas as pl
+from jax.experimental.pallas import tpu as pltpu
 from jax.sharding import PartitionSpec as P
+
 
 KVH = 8
 HD = 128
 BLK = 16
+F32 = jnp.float32
+BF16 = jnp.bfloat16
 
 
 def block_rows(prompt_blocks, prompt_row, total_blocks):
@@ -43,7 +48,7 @@
     return weighted / denominator[..., None]
 
 
-def on_device(prompt_x, decode_x, w_query, w_keyval, w_out, prompt_blocks, prompt_row):
+def general(prompt_x, decode_x, w_query, w_keyval, w_out, prompt_blocks, prompt_row):
     tp_count = lax.axis_size("tp")
     pool_count = lax.axis_size("pool")
     tp_index = lax.axis_index("tp")
@@ -77,19 +82,13 @@
     send_scale = jnp.where(to_half[None, :, :, None], scale_head[:, None], zero_value)
     got_vals, got_scale = (
         lax.all_to_all(
-            lax.all_to_all(send_vals, "tp", split_axis=0, concat_axis=0, tiled=True),
+            lax.all_to_all(sent, "tp", split_axis=0, concat_axis=0, tiled=True),
             "pool",
             split_axis=1,
             concat_axis=1,
             tiled=True,
-        ),
-        lax.all_to_all(
-            lax.all_to_all(send_scale, "tp", split_axis=0, concat_axis=0, tiled=True),
-            "pool",
-            split_axis=1,
-            concat_axis=1,
-            tiled=True,
-        ),
+        )
+        for sent in (send_vals, send_scale)
     )
     got_vals = got_vals.reshape(total_blocks, BLK, 2 * HD)
     got_scale = got_scale.reshape(total_blocks, 2)
@@ -99,7 +98,7 @@
         .reshape(total_blocks)
     )
     gathered = lax.all_gather(decode_x, "tp", axis=2, tiled=True)
-    step_count, row_count, model_width = gathered.shape
+    step_count, row_count, _ = gathered.shape
     heads_here = w_query.shape[1] // HD
     queries = jnp.einsum("srd,de->sre", gathered, w_query, preferred_element_type=jnp.float32)
     queries = queries.astype(jnp.bfloat16).reshape(step_count, row_count, heads_here, HD)
@@ -115,6 +114,429 @@
     return lax.psum_scatter(out_term, "tp", scatter_dimension=2, tiled=True).astype(jnp.bfloat16)
 
 
+VM = pl.BlockSpec(memory_space=pltpu.VMEM)
+SM = pl.BlockSpec(memory_space=pltpu.SMEM)
+HB = pl.BlockSpec(memory_space=pl.ANY)
+DMA = pltpu.SemaphoreType.DMA
+WIDE = 4 * HD
+FAR = (7, 6, 5, 4)
+NEAR = (3, 2, 1, 0)
+
+
+def struct(shape, dtype):
+    return jax.ShapeDtypeStruct(shape, dtype)
+
+
+def call(kernel, out_shape, in_specs, *args, scratch=(), mib=16, nbytes=2e6, flops=1e6):
+    single = not isinstance(out_shape, (list, tuple))
+    return pl.pallas_call(
+        kernel,
+        out_shape=out_shape,
+        in_specs=in_specs,
+        out_specs=VM if single else [VM] * len(out_shape),
+        scratch_shapes=list(scratch),
+        compiler_params=pltpu.CompilerParams(vmem_limit_bytes=mib << 20),
+        cost_estimate=pl.CostEstimate(
+            flops=int(flops), bytes_accessed=int(nbytes), transcendentals=0
+        ),
+    )(*args)
+
+
+def move(x, mask):
+    count = lax.axis_size("tp")
+    return lax.ppermute(x, "tp", [(i, i ^ mask) for i in range(count)])
+
+
+def dot(a, b):
+    return jnp.dot(a, b, preferred_element_type=F32)
+
+
+def start_all(copies):
+    for c in copies:
+        c.start()
+
+
+def wait_all(copies):
+    for c in copies:
+        c.wait()
+
+
+def pick_columns(w, blocks, width):
+    rows = w.shape[0]
+    count = blocks.shape[0]
+
+    def kernel(idx_ref, w_ref, o_ref, sem):
+        copies = [
+            pltpu.make_async_copy(
+                w_ref.at[:, pl.ds(pl.multiple_of(idx_ref[i] * width, width), width)],
+                o_ref.at[:, pl.ds(i * width, width)],
+                sem.at[i],
+            )
+            for i in range(count)
+        ]
+        start_all(copies)
+        wait_all(copies)
+
+    return call(
+        kernel,
+        struct((rows, count * width), w.dtype),
+        [SM, HB],
+        blocks,
+        w,
+        scratch=[DMA((count,))],
+        nbytes=4 * rows * count * width,
+    )
+
+
+def remote_terms(x, d, w, rows_a):
+    a = dot(x[:rows_a, :], w[:, WIDE:])
+    rest = jnp.concatenate([x[rows_a:, :], d[...]])
+    b = [dot(rest, w[:, j * WIDE + HD : (j + 1) * WIDE]) for j in range(2)]
+    return a, b
+
+
+def kv_before(x0, d0, w0, rows_a):
+    rows_b = x0.shape[0] - rows_a + d0.shape[0]
+
+    def kernel(x, d, w, a_ref, b_ref):
+        a, b = remote_terms(x, d, w, rows_a)
+        a_ref[...] = a
+        for j in range(2):
+            b_ref[:, j * 3 * HD : (j + 1) * 3 * HD] = b[j]
+
+    shapes = [struct((rows_a, WIDE), F32), struct((rows_b, 6 * HD), F32)]
+    return call(kernel, shapes, [VM] * 3, x0, d0, w0, mib=20)
+
+
+def kv_remote(pa, pb, x1, d0, d1, w1, rows_a):
+    fresh, depth = d0.shape
+    rows_b = pb.shape[0]
+    folds = depth // (2 * HD)
+
+    def kernel(pa, pb, x, d0, d1, w, a_ref, *b_refs):
+        a, b = remote_terms(x, d1, w, rows_a)
+        a_ref[...] = (pa[...] + a).astype(BF16)
+        for j in range(2):
+            t = (pb[:, j * 3 * HD : (j + 1) * 3 * HD] + b[j]).astype(BF16)
+            for k in range(3):
+                b_refs[k][:rows_b, j * HD : (j + 1) * HD] = t[:, k * HD : (k + 1) * HD]
+        for k in range(3):
+            for f in range(folds):
+                b_refs[k][rows_b + f * fresh : rows_b + (f + 1) * fresh, :] = d0[
+                    :, f * 2 * HD : (f + 1) * 2 * HD
+                ]
+
+    shapes = [struct((rows_a, WIDE), BF16)]
+    shapes += [struct((rows_b + folds * fresh, 2 * HD), BF16)] * 3
+    return call(kernel, shapes, [VM] * 6, pa, pb, x1, d0, d1, w1, mib=20)
+
+
+def kv_local(x0, x1, d0, d1, w0, w1, rows_a):
+    rows_b = x0.shape[0] - rows_a + d0.shape[0]
+
+    def kernel(x0, x1, d0, d1, w0, w1, a_ref, b_ref):
+        a_ref[...] = dot(x0[:rows_a, :], w0[:, :WIDE]) + dot(x1[:rows_a, :], w1[:, :WIDE])
+        rest0 = jnp.concatenate([x0[rows_a:, :], d0[...]])
+        rest1 = jnp.concatenate([x1[rows_a:, :], d1[...]])
+        for j in range(2):
+            cols = slice(j * WIDE, j * WIDE + HD)
+            b_ref[:, j * HD : (j + 1) * HD] = dot(rest0, w0[:, cols]) + dot(rest1, w1[:, cols])
+
+    shapes = [struct((rows_a, WIDE), F32), struct((rows_b, 2 * HD), F32)]
+    return call(kernel, shapes, [VM] * 6, x0, x1, d0, d1, w0, w1, mib=20)
+
+
+def mid_a(own, got):
+    rows = own.shape[0]
+
+    def kernel(own, got, m_ref, z1, z2, z3):
+        for k, ref in ((0, m_ref), (1, z1), (2, z2), (3, z3)):
+            cols = slice(k * HD, (k + 1) * HD)
+            ref[...] = (own[:, cols] + got[:, cols].astype(F32)).astype(ref.dtype)
+
+    shapes = [struct((rows, HD), F32)] + [struct((rows, HD), BF16)] * 3
+    return call(kernel, shapes, [VM] * 2, own, got)
+
+
+def mid_b(own, d0, g1, g2, g3):
+    rows = own.shape[0]
+    fresh, depth = d0.shape
+    folds = depth // HD
+
+    def kernel(own, d0, g1, g2, g3, m_ref, y_ref, s_ref):
+        for j, ref in ((0, m_ref), (1, y_ref)):
+            cols = slice(j * HD, (j + 1) * HD)
+            total = own[:, cols]
+            for g in (g1, g2, g3):
+                total = total + g[:rows, cols].astype(F32)
+            ref[:rows, :] = total.astype(ref.dtype)
+        for k in range(4):
+            for f in range(folds):
+                if k == 0:
+                    piece = d0[:, f * HD : (f + 1) * HD]
+                else:
+                    first = rows + f // 2 * fresh
+                    piece = (g1, g2, g3)[k - 1][
+                        first : first + fresh, f % 2 * HD : (f % 2 + 1) * HD
+                    ]
+                at = (k * folds + f) * fresh
+                y_ref[rows + at : rows + at + fresh, :] = piece
+                s_ref[at : at + fresh, :] = piece
+
+    span = 4 * folds * fresh
+    shapes = [struct((rows, HD), F32), struct((rows + span, HD), BF16), struct((span, HD), BF16)]
+    return call(kernel, shapes, [VM] * 5, own, d0, g1, g2, g3)
+
+
+def finish_kv(a_own, a1, a2, a3, b_own, b1, tokens):
+    rows_a, rows_b = a_own.shape[0], b_own.shape[0]
+    blocks = tokens // BLK
+    rows = rows_a + rows_b
+
+    def kernel(a_own, a1, a2, a3, b_own, b1, o_ref):
+        a = a_own[...] + a1[...].astype(F32) + a2[...].astype(F32) + a3[...].astype(F32)
+        b = b_own[...] + b1[:rows_b, :].astype(F32)
+        for v, first in ((a, 0), (b[: tokens - rows_a], rows_a)):
+            n = v.shape[0] // BLK
+            v = v.reshape(n, BLK, HD)
+            top = jnp.max(jnp.max(jnp.abs(v), axis=1, keepdims=True), axis=2, keepdims=True)
+            scale = (top + 1e-06).astype(BF16)
+            wide = jnp.broadcast_to(scale.astype(F32), (n, 1, HD))
+            o_ref[first : first + n * BLK, :] = (v / wide).astype(BF16).reshape(n * BLK, HD)
+            o_ref[rows + first // BLK : rows + first // BLK + n, :] = wide.reshape(n, HD).astype(
+                BF16
+            )
+        o_ref[tokens:rows, :] = b[tokens - rows_a :].astype(BF16)
+
+    shape = struct((rows + blocks, HD), BF16)
+    return call(kernel, shape, [VM] * 6, a_own, a1, a2, a3, b_own, b1)
+
+
+def queries_of(so, sx, first, side, rows, w_query, chip, core, acc=None):
+    cols = w_query.shape[1]
+    depth = w_query.shape[0] // 16
+    folds = depth // HD
+    starts = [(2 * (chip ^ (2 * k + side)) + (core ^ o)) * depth for k in range(4) for o in range(2)]
+    starts = jnp.stack(starts).astype(jnp.int32)
+
+    def kernel(idx, so, sx, w_ref, *rest):
+        out, wbuf, sem = rest[-3:]
+        copies = [
+            pltpu.make_async_copy(
+                w_ref.at[pl.ds(pl.multiple_of(idx[i], depth), depth), :], wbuf.at[i], sem.at[i]
+            )
+            for i in range(8)
+        ]
+        start_all(copies)
+        total = rest[0][...] if acc is not None else jnp.zeros((rows, cols), F32)
+        for k in range(4):
+            for o, s in ((0, so), (1, sx)):
+                lhs = jnp.concatenate(
+                    [
+                        s[first + (k * folds + f) * rows : first + (k * folds + f + 1) * rows, :]
+                        for f in range(folds)
+                    ],
+                    axis=1,
+                )
+                copies[2 * k + o].wait()
+                total = total + dot(lhs, wbuf[2 * k + o])
+        out[...] = total.astype(out.dtype)
+
+    extra = [] if acc is None else [acc]
+    return call(
+        kernel,
+        struct((rows, cols), F32 if acc is None else BF16),
+        [SM, VM, VM, HB] + [VM] * len(extra),
+        starts,
+        so,
+        sx,
+        w_query,
+        *extra,
+        scratch=[pltpu.VMEM((8, depth, cols), BF16), DMA((8,))],
+        nbytes=5e6,
+        flops=3e8,
+    )
+
+
+def weight_copies(idx, w_out, w_got, wbuf, sem, first):
+    width = wbuf.shape[-1]
+    copies = []
+    for i in range(4):
+        column = pl.ds(pl.multiple_of(idx[i] * width, width), width)
+        copies.append(pltpu.make_async_copy(w_out.at[:, column], wbuf.at[i, 0], sem.at[i, 0]))
+        column = pl.ds((first + i) * width, width)
+        copies.append(pltpu.make_async_copy(w_got.at[:, column], wbuf.at[i, 1], sem.at[i, 1]))
+    return copies
+
+
+def weight_scratch(w_out, width):
+    return [pltpu.VMEM((4, 2, w_out.shape[0], width), BF16), DMA((4, 2))]
+
+
+def attend_far(q0, q1, kv0, kv1, marks, w_out, w_got, chip, core, tokens, row_count):
+    rows, qcols = q0.shape
+    heads = qcols // HD
+    blocks = tokens // BLK
+    slots = tokens + rows
+    width = w_got.shape[1] // 8
+    rate = math.log2(math.e) / math.sqrt(HD)
+    order = jnp.stack([2 * (chip ^ r) + core for r in FAR] + [core]).astype(jnp.int32)
+
+    def kernel(idx, q0, q1, kv0, kv1, mk, w_out, w_got, att0, att1, *rest):
+        outs, wbuf, sem = rest[:4], rest[4], rest[5]
+        copies = weight_copies(idx, w_out, w_got, wbuf, sem, 0)
+        start_all(copies)
+        first = idx[4] == 0
+
+        def wide(kv):
+            scale = kv[slots:, :].astype(F32).reshape(blocks, 1, HD)
+            v = kv[:tokens, :].astype(F32).reshape(blocks, BLK, HD) * scale
+            return v.reshape(tokens, HD).astype(BF16)
+
+        own, oth = wide(kv0), wide(kv1)
+        own_new, oth_new = kv0[tokens:slots, :], kv1[tokens:slots, :]
+        keys = jnp.concatenate([jnp.where(first, own, oth), jnp.where(first, own_new, oth_new)])
+        values = jnp.concatenate([jnp.where(first, oth, own), jnp.where(first, oth_new, own_new)])
+        who = lax.broadcasted_iota(jnp.int32, (rows, slots), 0)
+        seen = (lax.rem(who, row_count) == mk[0:1, :]) & (who >= mk[1:2, :])
+        for q, att in ((q0, att0), (q1, att1)):
+            stack = jnp.concatenate([q[:, g * HD : (g + 1) * HD] for g in range(heads)])
+            score = lax.dot_general(
+                stack, keys, (((1,), (1,)), ((), ())), preferred_element_type=F32
+            )
+            score = jnp.where(seen[None], score.reshape(heads, rows, slots), -jnp.inf)
+            top = jnp.max(score, axis=2, keepdims=True)
+            weight = jnp.exp2((score - top) * rate)
+            total = jnp.sum(weight, axis=2, keepdims=True)
+            mixed = dot(weight.astype(BF16).reshape(heads * rows, slots), values)
+            mixed = mixed.reshape(heads, rows, HD) / total
+            for g in range(heads):
+                att[:, g * HD : (g + 1) * HD] = mixed[g].astype(BF16)
+        for i in range(4):
+            wait_all(copies[2 * i : 2 * i + 2])
+            term = dot(att0[...], wbuf[i, 0]) + dot(att1[...], wbuf[i, 1])
+            outs[i][...] = term.astype(BF16)
+
+    shapes = [struct((rows, qcols), BF16)] * 2 + [struct((rows, width), BF16)] * 4
+    return call(
+        kernel,
+        shapes,
+        [SM] + [VM] * 5 + [HB] * 2,
+        order,
+        q0,
+        q1,
+        kv0,
+        kv1,
+        marks,
+        w_out,
+        w_got,
+        scratch=weight_scratch(w_out, width),
+        mib=32,
+        flops=8e8,
+        nbytes=5e6,
+    )
+
+
+def out_near(att0, att1, w_out, w_got, chip, core):
+    rows = att0.shape[0]
+    width = w_got.shape[1] // 8
+    order = jnp.stack([2 * (chip ^ r) + core for r in NEAR]).astype(jnp.int32)
+
+    def kernel(idx, att0, att1, w_out, w_got, *rest):
+        outs, wbuf, sem = rest[:4], rest[4], rest[5]
+        copies = weight_copies(idx, w_out, w_got, wbuf, sem, 4)
+        start_all(copies)
+        for i in range(4):
+            wait_all(copies[2 * i : 2 * i + 2])
+            term = dot(att0[...], wbuf[i, 0]) + dot(att1[...], wbuf[i, 1])
+            outs[i][...] = term.astype(outs[i].dtype)
+
+    shapes = [struct((rows, width), BF16)] * 3 + [struct((rows, width), F32)]
+    return call(
+        kernel,
+        shapes,
+        [SM, VM, VM, HB, HB],
+        order,
+        att0,
+        att1,
+        w_out,
+        w_got,
+        scratch=weight_scratch(w_out, width),
+        flops=5e8,
+        nbytes=5e6,
+    )
+
+
+def add_up(own, parts):
+    def kernel(*refs):
+        total = refs[0][...]
+        for r in refs[1:-1]:
+            total = total + r[...].astype(F32)
+        refs[-1][...] = total.astype(BF16)
+
+    return call(kernel, struct(own.shape, BF16), [VM] * (1 + len(parts)), own, *parts)
+
+
+def paired(prompt_x, decode_x, w_query, w_keyval, w_out, prompt_blocks, prompt_row):
+    return paired_body(
+        prompt_x, decode_x, w_query, w_keyval, w_out, prompt_blocks, prompt_row
+    )
+
+
+def paired_body(prompt_x, decode_x, w_query, w_keyval, w_out, prompt_blocks, prompt_row):
+    count = lax.axis_size("tp")
+    index = lax.axis_index("tp")
+    core, chip = index % 2, index // 2
+    tokens = prompt_x.shape[0]
+    steps, row_count, depth = decode_x.shape
+    fresh = steps * row_count
+    total_blocks = tokens // BLK
+    rows_a = (tokens + fresh) * 3 // 4 // BLK * BLK
+    rows_b = tokens - rows_a + fresh
+    d_own = decode_x.reshape(fresh, depth)
+    x_oth = move(prompt_x, 1)
+    d_oth = move(d_own, 1)
+    rel = [(i % 4) * 2 + i // 4 for i in range(8)]
+    keep_cols = jnp.stack([(chip ^ r) * 2 + core for r in rel]).astype(jnp.int32)
+    send_cols = jnp.stack([(chip ^ r) * 2 + 1 - core for r in rel]).astype(jnp.int32)
+    w_oth = move(pick_columns(w_keyval, send_cols, HD), 1)
+    w_keep = pick_columns(w_keyval, keep_cols, HD)
+    pa, pb = kv_before(prompt_x, d_own, w_keep, rows_a)
+    a_send, b1, b2, b3 = kv_remote(pa, pb, x_oth, d_own, d_oth, w_oth, rows_a)
+    a_got = move(a_send, 2)
+    g2, g3, g1 = move(b2, 8), move(b3, 12), move(b1, 4)
+    a_own, b_own = kv_local(prompt_x, x_oth, d_own, d_oth, w_keep, w_oth, rows_a)
+    width = w_out.shape[1] // count
+    out_cols = jnp.stack([2 * (chip ^ r) + 1 - core for r in FAR + NEAR]).astype(jnp.int32)
+    w_got = move(pick_columns(w_out, out_cols, width), 1)
+    a_own, a1, a2, a3 = mid_a(a_own, a_got)
+    h2 = move(a2, 8)
+    b_own, y_send, s0 = mid_b(b_own, d_own, g1, g2, g3)
+    y_got = move(y_send, 2)
+    h3, h1 = move(a3, 12), move(a1, 4)
+    s0_oth = move(s0, 1)
+    acc = queries_of(s0, s0_oth, 0, 0, fresh, w_query, chip, core)
+    y_oth = move(y_got, 1)
+    q_own = queries_of(y_got, y_oth, rows_b, 1, fresh, w_query, chip, core, acc)
+    q_oth = move(q_own, 1)
+    slot_row = jnp.repeat(block_rows(prompt_blocks, prompt_row, total_blocks), BLK)
+    new = jnp.arange(fresh, dtype=jnp.int32)
+    marks = jnp.stack(
+        [
+            jnp.concatenate([slot_row, new % row_count]),
+            jnp.concatenate([jnp.zeros_like(slot_row), new // row_count * row_count]),
+        ]
+    )
+    kv_own = finish_kv(a_own, h1, h2, h3, b_own, y_got, tokens)
+    kv_oth = move(kv_own, 1)
+    att0, att1, *far = attend_far(
+        q_own, q_oth, kv_own, kv_oth, marks, w_out, w_got, chip, core, tokens, row_count
+    )
+    *near, mine = out_near(att0, att1, w_out, w_got, chip, core)
+    parts = [move(s, 2 * r) for r, s in zip(FAR + NEAR, far + near)]
+    return add_up(mine, parts).reshape(steps, row_count, width)
+
+
 def solution(mesh):
     placed = (
         P(("group", "pool"), "tp"),
@@ -125,8 +547,9 @@
         P("group"),
         P("group"),
     )
+    pairs = mesh.shape["pool"] == 1 and mesh.shape["tp"] == 2 * KVH
     return jax.shard_map(
-        on_device,
+        paired if pairs else general,
         mesh=mesh,
         in_specs=placed,
         out_specs=P(None, ("group", "pool"), "tp"),

time: 255 us -> 110 us (0.43)
  waiting for transfers between devices: 120 us -> 39 us
  blocking collectives: 74.8 us -> 0 us
  Pallas kernels: 0 us -> 29.7 us
  matrix products: 24 us -> 0 us
  starting transfers between devices: 7.99 us -> 27.9 us
  between operations: 13.3 us -> 0.22 us
  other arithmetic: 7.65 us -> 0.43 us
  local copies, waits for them, and re-layouts: 6.69 us -> 12.7 us
    reduce_scatter x2 -> x0, waiting for transfers between devices: 93.3 us -> none  [the longest x1 61.2 us: on_device(): lax.psum_scatter(out_term, 'tp', scatter_dimension=2, tiled=True)]
    psum x1 -> x0, blocking collectives: 74.8 us -> none  [on_device(): summed_new = lax.psum(partial_new, 'tp')]
    ppermute x0 -> x23, waiting for transfers between devices: none -> 39 us  [move(): return lax.ppermute(x, 'tp', [(i, i ^ mask) for i in range(count)])]
    pallas_call x0 -> x14, Pallas kernels: none -> 29.7 us  [call(): pl.pallas_call(kernel, out_shape=out_shape, in_specs=in_specs, out_specs=...]
    ppermute x0 -> x23, starting transfers between devices: none -> 27.9 us  [move(): return lax.ppermute(x, 'tp', [(i, i ^ mask) for i in range(count)])]
    dot_general x8 -> x0, matrix products: 24 us -> none  [the longest x1 6.79 us: on_device(): jnp.dot(prompt_x, w_keyval, preferred_element_type=jnp.float32)]
    all_gather x1 -> x0, waiting for transfers between devices: 20.9 us -> none  [on_device(): gathered = lax.all_gather(decode_x, 'tp', axis=2, tiled=True)]
    unnamed x14 -> x22, local copies, waits for them, and re-layouts: 1.87 us -> 11.9 us
  transfers between devices with their start and end apart: 5 -> 23, of which waited for: 4 -> 9; matrix products, arithmetic and copies ran while one was open for 6% -> 1% of each run, Pallas kernels for 0% -> 17%
where the time goes in v1:
time: 110 us
  waiting for transfers between devices  39 us (35%)
  Pallas kernels  29.7 us (27%)
  starting transfers between devices  27.9 us (25%)
  local copies, waits for them, and re-layouts  12.7 us (12%)
    ppermute x23, waiting for transfers between devices, move(): return lax.ppermute(x, 'tp', [(i, i ^ mask) for i in range(count)])  39 us
    pallas_call x14, Pallas kernels, call(): pl.pallas_call(kernel, out_shape=out_shape, in_specs=in_specs, out_specs=...  29.7 us
    ppermute x23, starting transfers between devices, move(): return lax.ppermute(x, 'tp', [(i, i ^ mask) for i in range(count)])  27.9 us
    unnamed x22, local copies, waits for them, and re-layouts  11.9 us
  transfers between devices with their start and end apart: 23, of which 9 were waited for; matrix products, arithmetic and copies ran while one was open for 1% of the time, Pallas kernels for 17%

profile of v1, /device:TPU:0, one launch (start us, length us, event | category | flops | bytes accessed | tf_op | source)
XLA Modules:
  0.0 110.0 jit_solution(4273974973243205667)
XLA Ops:
  0.0 0.1 stack.187.idx_ref
  0.1 3.4 %copy-done = bf16[512,8192]{1,0:T(8,128)(2,1)S(1)} copy-done((bf16[512,8192]{1,0:T(8,128)(2,1)S(1)}, bf16[512,8192]{1,0:T(8,128)(2,1)}, u32[]{:S(2)}) %copy-start) | copy-done | bytes 8388632
  3.5 3.2 %shard_map.83 = bf16[512,4096]{1,0:T(8,128)(2,1)} custom-call(s32[8]{0:T(128)S(1)} %stack.187.idx_ref, bf16[512,8192]{1,0:T(8,128)(2,1)S(1)} %copy-done), custom_call_target="tpu_custom_call" | custom-call | flops 1000000 | bytes 8388608 | tf_op jit(solution)/shard_map/pallas_call | solution.py:132
  6.6 0.6 collective-permute-start.15
  7.2 0.1 stack.174.idx_ref
  7.3 1.9 %shard_map.74 = bf16[512,1024]{1,0:T(8,128)(2,1)} custom-call(s32[8]{0:T(128)S(1)} %stack.174.idx_ref, bf16[512,2048]{1,0:T(8,128)(2,1)S(1)} %copy-done.3), custom_call_target="tpu_custom_call" | custom-call | flops 1000000 | bytes 2097152 | tf_op jit(solution)/shard_map/pallas_call | solution.py:132
  9.2 0.1 collective-permute-start.2
  9.3 0.5 collective-permute-start
  9.8 0.1 collective-permute-start.1
  9.9 0.1 stack.165.idx_ref
  9.9 0.9 shard_map.73.w0.w
  10.9 0.0 copy-start.7
  10.9 2.1 %shard_map.76 = (f32[816,512]{1,0:T(8,128)S(1)}, f32[272,768]{1,0:T(8,128)S(1)}) custom-call(bf16[1024,512]{1,0:T(8,128)(2,1)} %x.3, bf16[64,512]{1,0:T(8,128)(2,1)S(1)} %bitcast.39, bf16[512,1024]{1,0:T(8,128)(2,1)S(1)} %shard_map.73.w0.w), custom_call_target="tpu_custom_call" | custom-call | flops 1000000 | bytes 2000000 | tf_op jit(solution)/shard_map/pallas_call | solution.py:132
  13.0 4.3 %collective-permute-done.1.d1 = bf16[64,512]{1,0:T(8,128)(2,1)S(1)} collective-permute-done((bf16[64,512]{1,0:T(8,128)(2,1)S(1)}, bf16[64,512]{1,0:T(8,128)(2,1)S(1)}, u32[]{:S(2)}, u32[]{:S(2)}) %collective-permute-start.1) | collective-permute-done | bytes 65568 | tf_op jit(solution)/shard_map/ppermute | solution.py:147
  17.3 3.3 %shard_map.77 = (bf16[816,512]{1,0:T(8,128)(2,1)}, bf16[400,256]{1,0:T(8,128)(2,1)}, bf16[400,256]{1,0:T(8,128)(2,1)}, bf16[400,256]{1,0:T(8,128)(2,1)}) custom-call(f32[816,512]{1,0:T(8,128)S(1)} %get-tuple-element.31.pa, f32[272,768]{1,0:T(8,128)S(1)} %get-tuple-element.32.pb, bf16[1024,512]{1,0:T(8,128)(2,1)} %collective-permute-done.x1.x, ...), custom_call_target="tpu_custom_call" | custom-call | flops 1000000 | bytes 2000000 | tf_op jit(solution)/shard_map/pallas_call | solution.py:132
  20.6 2.9 %collective-permute-start.10 = (bf16[816,512]{1,0:T(8,128)(2,1)}, bf16[816,512]{1,0:T(8,128)(2,1)}, u32[]{:S(2)}, u32[]{:S(2)}) collective-permute-start(bf16[816,512]{1,0:T(8,128)(2,1)} %get-tuple-element.39), channel_id=1, source_target_pairs={{0,2},{1,3},{2,0},{3,1},{4,6},{5,7},{6,4},{7,5},{8,10},{9,11},{10,... | collective-permute-start | bytes 2506760 | tf_op jit(solution)/shard_map/ppermute | solution.py:147
  23.5 1.6 %collective-permute-start.3 = (bf16[400,256]{1,0:T(8,128)(2,1)}, bf16[400,256]{1,0:T(8,128)(2,1)S(1)}, u32[]{:S(2)}, u32[]{:S(2)}) collective-permute-start(bf16[400,256]{1,0:T(8,128)(2,1)} %get-tuple-element.33), channel_id=1, source_target_pairs={{0,4},{1,5},{2,6},{3,7},{4,0},{5,1},{6,2},{7,3},{8,12},{9,13},{10,... | collective-permute-start | bytes 614408 | tf_op jit(solution)/shard_map/ppermute | solution.py:147
  25.1 2.6 %collective-permute-start.4 = (bf16[400,256]{1,0:T(8,128)(2,1)}, bf16[400,256]{1,0:T(8,128)(2,1)}, u32[]{:S(2)}, u32[]{:S(2)}) collective-permute-start(bf16[400,256]{1,0:T(8,128)(2,1)} %get-tuple-element.34), channel_id=1, source_target_pairs={{0,8},{1,9},{2,10},{3,11},{4,12},{5,13},{6,14},{7,15},{8,0},{9,1},... | collective-permute-start | bytes 614408 | tf_op jit(solution)/shard_map/ppermute | solution.py:147
  27.7 0.2 collective-permute-start.5
  27.9 0.1 copy.10
  28.0 0.1 reduce
  28.2 0.1 convert_reduce_fusion
  28.2 3.2 %shard_map.75 = (f32[816,512]{1,0:T(8,128)S(1)}, f32[272,256]{1,0:T(8,128)S(1)}) custom-call(bf16[1024,512]{1,0:T(8,128)(2,1)} %x.3, bf16[1024,512]{1,0:T(8,128)(2,1)} %collective-permute-done.x1.x, bf16[64,512]{1,0:T(8,128)(2,1)S(1)} %bitcast.41, bf16[64,512]{1,0:T(8,128)(2,1)S(1)} %collective-permute-done.1.d1, bf16[512,1024]{1,0:T(8,128)(2,1)S(1)} %shard_map.73.w0.w, ...), custom_call_target="tpu_custom_call" | custom-call | flops 1000000 | bytes 2000000 | tf_op jit(solution)/shard_map/pallas_call | solution.py:132
  31.4 2.8 %collective-permute-done.3.g1 = bf16[400,256]{1,0:T(8,128)(2,1)S(1)} collective-permute-done((bf16[400,256]{1,0:T(8,128)(2,1)}, bf16[400,256]{1,0:T(8,128)(2,1)S(1)}, u32[]{:S(2)}, u32[]{:S(2)}) %collective-permute-start.3) | collective-permute-done | bytes 204832 | tf_op jit(solution)/shard_map/ppermute | solution.py:147
  34.2 0.7 copy-done.5
  34.9 8.1 %collective-permute-done.4.g2 = bf16[400,256]{1,0:T(8,128)(2,1)} collective-permute-done((bf16[400,256]{1,0:T(8,128)(2,1)}, bf16[400,256]{1,0:T(8,128)(2,1)}, u32[]{:S(2)}, u32[]{:S(2)}) %collective-permute-start.4) | collective-permute-done | bytes 204832 | tf_op jit(solution)/shard_map/ppermute | solution.py:147
  43.0 0.9 copy-done.6
  44.0 1.9 %shard_map.78 = (f32[272,128]{1,0:T(8,128)S(1)}, bf16[1296,128]{1,0:T(8,128)(2,1)}, bf16[1024,128]{1,0:T(8,128)(2,1)S(1)}) custom-call(f32[272,256]{1,0:T(8,128)S(1)} %get-tuple-element.30.own, bf16[64,512]{1,0:T(8,128)(2,1)S(1)} %bitcast.42, bf16[400,256]{1,0:T(8,128)(2,1)S(1)} %copy-done.6, bf16[400,256]{1,0:T(8,128)(2,1)} %collective-permute-done.4.g2, ...), custom_call_target="tpu_custom_call" | custom-call | flops 1000000 | bytes 2000000 | tf_op jit(solution)/shard_map/pallas_call | solution.py:132
  45.9 0.5 collective-permute-start.6
  46.4 0.1 select_reduce_fusion
  46.5 0.1 broadcast_in_dim.23
  46.5 0.1 reshape.38
  46.6 1.9 %shard_map.81 = (f32[816,128]{1,0:T(8,128)S(1)}, bf16[816,128]{1,0:T(8,128)(2,1)S(1)}, bf16[816,128]{1,0:T(8,128)(2,1)}, bf16[816,128]{1,0:T(8,128)(2,1)S(1)}) custom-call(f32[816,512]{1,0:T(8,128)S(1)} %get-tuple-element.38.own, bf16[816,512]{1,0:T(8,128)(2,1)} %collective-permute-done.10.got), custom_call_target="tpu_custom_call" | custom-call | flops 1000000 | bytes 2000000 | tf_op jit(solution)/shard_map/pallas_call | solution.py:132
  48.5 3.6 %collective-permute-start.11 = (bf16[816,128]{1,0:T(8,128)(2,1)S(1)}, bf16[816,128]{1,0:T(8,128)(2,1)S(1)}, u32[]{:S(2)}, u32[]{:S(2)}) collective-permute-start(bf16[816,128]{1,0:T(8,128)(2,1)S(1)} %get-tuple-element.41), channel_id=1, source_target_pairs={{0,4},{1,5},{2,6},{3,7},{4,0},{5,1},{6,2},{7,3},{8,12},{9,13},{10,... | collective-permute-start | bytes 626696 | tf_op jit(solution)/shard_map/ppermute | solution.py:147
  52.1 1.0 collective-permute-start.12
  53.1 1.5 %collective-permute-start.13 = (bf16[816,128]{1,0:T(8,128)(2,1)S(1)}, bf16[816,128]{1,0:T(8,128)(2,1)S(1)}, u32[]{:S(2)}, u32[]{:S(2)}) collective-permute-start(bf16[816,128]{1,0:T(8,128)(2,1)S(1)} %get-tuple-element.43), channel_id=1, source_target_pairs={{0,12},{1,13},{2,14},{3,15},{4,8},{5,9},{6,10},{7,11},{8,4},{9,5},... | collective-permute-start | bytes 626696 | tf_op jit(solution)/shard_map/ppermute | solution.py:147
  54.6 4.0 %collective-permute-done.11.a1 = bf16[816,128]{1,0:T(8,128)(2,1)S(1)} collective-permute-done((bf16[816,128]{1,0:T(8,128)(2,1)S(1)}, bf16[816,128]{1,0:T(8,128)(2,1)S(1)}, u32[]{:S(2)}, u32[]{:S(2)}) %collective-permute-start.11) | collective-permute-done | bytes 208928 | tf_op jit(solution)/shard_map/ppermute | solution.py:147
  58.6 0.1 stack.155.idx
  58.7 0.1 stack.183.idx
  58.8 0.1 stack.164.idx
  58.9 10.7 %collective-permute-done.12.a2 = bf16[816,128]{1,0:T(8,128)(2,1)S(1)} collective-permute-done((bf16[816,128]{1,0:T(8,128)(2,1)}, bf16[816,128]{1,0:T(8,128)(2,1)S(1)}, u32[]{:S(2)}, u32[]{:S(2)}) %collective-permute-start.12) | collective-permute-done | bytes 208928 | tf_op jit(solution)/shard_map/ppermute | solution.py:147
  69.6 0.3 shard_map.82.kv0
  69.9 0.1 collective-permute-start.14
  70.0 0.0 copy-start.1
  70.0 3.4 %copy-done.1 = bf16[8192,512]{1,0:T(8,128)(2,1)S(1)} copy-done((bf16[8192,512]{1,0:T(8,128)(2,1)S(1)}, bf16[8192,512]{1,0:T(8,128)(2,1)}, u32[]{:S(2)}) %copy-start.1) | copy-done | bytes 8388632
  73.4 1.9 %shard_map.79.rest_0_ = f32[64,512]{1,0:T(8,128)S(1)} custom-call(s32[8]{0:T(128)S(1)} %stack.183.idx, bf16[1024,128]{1,0:T(8,128)(2,1)S(1)} %get-tuple-element.37.so, bf16[1024,128]{1,0:T(8,128)(2,1)S(1)} %collective-permute-done.8.sx, bf16[8192,512]{1,0:T(8,128)(2,1)S(1)} %copy-done.1), custom_call_target="tpu_custom_call" | custom-call | flops 300000000 | bytes 5000000 | tf_op jit(solution)/shard_map/pallas_call | solution.py:132
  75.3 0.0 slice-start.1
  75.3 3.5 %copy-done.2 = bf16[8192,512]{1,0:T(8,128)(2,1)S(1)} copy-done((bf16[8192,512]{1,0:T(8,128)(2,1)S(1)}, bf16[8192,512]{1,0:T(8,128)(2,1)}, u32[]{:S(2)}) %copy-start.2) | copy-done | bytes 8388632
  78.9 1.9 %shard_map.80.q0 = bf16[64,512]{1,0:T(8,128)(2,1)S(1)} custom-call(s32[8]{0:T(128)S(1)} %stack.164.idx, bf16[1296,128]{1,0:T(8,128)(2,1)S(1)} %collective-permute-done.6.so.b1, bf16[1296,128]{1,0:T(8,128)(2,1)S(1)} %collective-permute-done.7.sx, bf16[8192,512]{1,0:T(8,128)(2,1)S(1)} %copy-done.2, f32[64,512]{1,0:T(8,128)S(1)} %shard_map.79.rest_0_), custom_call_target="tpu_custom_call" | custom-call | flops 300000000 | bytes 5000000 | tf_op jit(solution)/shard_map/pallas_call | solution.py:132
  80.8 0.6 collective-permute-start.9
  81.3 0.1 pad_add_fusion.2.idx
  81.4 0.8 collective-permute-done.9.q1
  82.3 3.6 %shard_map.84 = (bf16[64,512]{1,0:T(8,128)(2,1)S(1)}, bf16[64,512]{1,0:T(8,128)(2,1)S(1)}, bf16[64,512]{1,0:T(8,128)(2,1)S(1)}, bf16[64,512]{1,0:T(8,128)(2,1)S(...) custom-call(s32[5]{0:T(128)S(1)} %stack.155.idx, bf16[64,512]{1,0:T(8,128)(2,1)S(1)} %shard_map.80.q0, ...), custom_call_target="tpu_custom_call" | custom-call | flops 800000000 | bytes 5000000 | tf_op jit(solution)/shard_map/pallas_call | solution.py:132
  85.9 2.9 %shard_map.85 = (bf16[64,512]{1,0:T(8,128)(2,1)S(1)}, bf16[64,512]{1,0:T(8,128)(2,1)S(1)}, bf16[64,512]{1,0:T(8,128)(2,1)S(1)}, f32[64,512]{1,0:T(8,128)S(1)}) custom-call(s32[4]{0:T(128)S(1)} %pad_add_fusion.2.idx, bf16[64,512]{1,0:T(8,128)(2,1)S(1)} %get-tuple-element.45.att0, bf16[64,512]{1,0:T(8,128)(2,1)S(1)} %get-tuple-element.46.att1, ...), custom_call_target="tpu_custom_call" | custom-call | flops 500000000 | bytes 5000000 | tf_op jit(solution)/shard_map/pallas_call | solution.py:132
  88.9 3.9 %collective-permute-start.20 = (bf16[64,512]{1,0:T(8,128)(2,1)S(1)}, bf16[64,512]{1,0:T(8,128)(2,1)S(1)}, u32[]{:S(2)}, u32[]{:S(2)}) collective-permute-start(bf16[64,512]{1,0:T(8,128)(2,1)S(1)} %get-tuple-element.52), channel_id=1, source_target_pairs={{0,6},{1,7},{2,4},{3,5},{4,2},{5,3},{6,0},{7,1},{8,14},{9,15},{10,... | collective-permute-start | bytes 196616 | tf_op jit(solution)/shard_map/ppermute | solution.py:147
  92.8 0.6 collective-permute-start.22
  93.4 3.2 %collective-permute-start.16 = (bf16[64,512]{1,0:T(8,128)(2,1)S(1)}, bf16[64,512]{1,0:T(8,128)(2,1)S(1)}, u32[]{:S(2)}, u32[]{:S(2)}) collective-permute-start(bf16[64,512]{1,0:T(8,128)(2,1)S(1)} %get-tuple-element.48), channel_id=1, source_target_pairs={{0,14},{1,15},{2,12},{3,13},{4,10},{5,11},{6,8},{7,9},{8,6},{9,7},... | collective-permute-start | bytes 196616 | tf_op jit(solution)/shard_map/ppermute | solution.py:147
  96.7 1.4 %collective-permute-start.17 = (bf16[64,512]{1,0:T(8,128)(2,1)S(1)}, bf16[64,512]{1,0:T(8,128)(2,1)S(1)}, u32[]{:S(2)}, u32[]{:S(2)}) collective-permute-start(bf16[64,512]{1,0:T(8,128)(2,1)S(1)} %get-tuple-element.49), channel_id=1, source_target_pairs={{0,12},{1,13},{2,14},{3,15},{4,8},{5,9},{6,10},{7,11},{8,4},{9,5},... | collective-permute-start | bytes 196616 | tf_op jit(solution)/shard_map/ppermute | solution.py:147
  98.1 1.5 %collective-permute-start.18 = (bf16[64,512]{1,0:T(8,128)(2,1)S(1)}, bf16[64,512]{1,0:T(8,128)(2,1)S(1)}, u32[]{:S(2)}, u32[]{:S(2)}) collective-permute-start(bf16[64,512]{1,0:T(8,128)(2,1)S(1)} %get-tuple-element.50), channel_id=1, source_target_pairs={{0,10},{1,11},{2,8},{3,9},{4,14},{5,15},{6,12},{7,13},{8,2},{9,3},... | collective-permute-start | bytes 196616 | tf_op jit(solution)/shard_map/ppermute | solution.py:147
  99.6 1.5 %collective-permute-start.19 = (bf16[64,512]{1,0:T(8,128)(2,1)S(1)}, bf16[64,512]{1,0:T(8,128)(2,1)S(1)}, u32[]{:S(2)}, u32[]{:S(2)}) collective-permute-start(bf16[64,512]{1,0:T(8,128)(2,1)S(1)} %get-tuple-element.51), channel_id=1, source_target_pairs={{0,8},{1,9},{2,10},{3,11},{4,12},{5,13},{6,14},{7,15},{8,0},{9,1},... | collective-permute-start | bytes 196616 | tf_op jit(solution)/shard_map/ppermute | solution.py:147
  101.1 1.6 %collective-permute-done.17.refs_2_ = bf16[64,512]{1,0:T(8,128)(2,1)S(1)} collective-permute-done((bf16[64,512]{1,0:T(8,128)(2,1)S(1)}, bf16[64,512]{1,0:T(8,128)(2,1)S(1)}, u32[]{:S(2)}, u32[]{:S(2)}) %collective-permute-start.17) | collective-permute-done | bytes 65568 | tf_op jit(solution)/shard_map/ppermute | solution.py:147
  102.7 5.8 %collective-permute-done.18.refs_3_ = bf16[64,512]{1,0:T(8,128)(2,1)S(1)} collective-permute-done((bf16[64,512]{1,0:T(8,128)(2,1)S(1)}, bf16[64,512]{1,0:T(8,128)(2,1)S(1)}, u32[]{:S(2)}, u32[]{:S(2)}) %collective-permute-start.18) | collective-permute-done | bytes 65568 | tf_op jit(solution)/shard_map/ppermute | solution.py:147
  108.6 0.7 collective-permute-done.19.refs_4_
  109.3 0.7 shard_map.86
  (40 shorter events, 0.1 us)
Async XLA Ops:
  0.1 3.4 %copy-start = (bf16[512,8192]{1,0:T(8,128)(2,1)S(1)}, bf16[512,8192]{1,0:T(8,128)(2,1)}, u32[]{:S(2)}) copy-start(bf16[512,8192]{1,0:T(8,128)(2,1)} %w_out.3) | copy-start | bytes 25165828
  3.5 3.8 %copy-start.3 = (bf16[512,2048]{1,0:T(8,128)(2,1)S(1)}, bf16[512,2048]{1,0:T(8,128)(2,1)}, u32[]{:S(2)}) copy-start(bf16[512,2048]{1,0:T(8,128)(2,1)} %w_ref.6) | copy-start | bytes 6291460
  3.5 6.3 %copy-start.4 = (bf16[4,16,512]{2,1,0:T(8,128)(2,1)S(1)}, bf16[4,16,512]{2,1,0:T(8,128)(2,1)}, u32[]{:S(2)}) copy-start(bf16[4,16,512]{2,1,0:T(8,128)(2,1)} %param.8) | copy-start | bytes 196612
  6.6 75.6 %collective-permute-start.15 = (bf16[512,4096]{1,0:T(8,128)(2,1)}, bf16[512,4096]{1,0:T(8,128)(2,1)}, u32[]{:S(2)}, u32[]{:S(2)}) collective-permute-start(bf16[512,4096]{1,0:T(8,128)(2,1)} %shard_map.83), channel_id=1, source_target_pairs={{0,1},{1,0},{2,3},{3,2},{4,5},{5,4},{6,7},{7,6},{8,9},{9,8},{10,11... | collective-permute-start | bytes 12582920 | tf_op jit(solution)/shard_map/ppermute | solution.py:147
  9.2 8.1 %collective-permute-start.2 = (bf16[512,1024]{1,0:T(8,128)(2,1)}, bf16[512,1024]{1,0:T(8,128)(2,1)}, u32[]{:S(2)}, u32[]{:S(2)}) collective-permute-start(bf16[512,1024]{1,0:T(8,128)(2,1)} %shard_map.74), channel_id=1, source_target_pairs={{0,1},{1,0},{2,3},{3,2},{4,5},{5,4},{6,7},{7,6},{8,9},{9,8},{10,11... | collective-permute-start | bytes 3145736 | tf_op jit(solution)/shard_map/ppermute | solution.py:147
  9.3 8.1 %collective-permute-start = (bf16[1024,512]{1,0:T(8,128)(2,1)}, bf16[1024,512]{1,0:T(8,128)(2,1)}, u32[]{:S(2)}, u32[]{:S(2)}) collective-permute-start(bf16[1024,512]{1,0:T(8,128)(2,1)} %x.3), channel_id=1, source_target_pairs={{0,1},{1,0},{2,3},{3,2},{4,5},{5,4},{6,7},{7,6},{8,9},{9,8},{10,11... | collective-permute-start | bytes 3145736 | tf_op jit(solution)/shard_map/ppermute | solution.py:147
  9.8 7.5 %collective-permute-start.1 = (bf16[64,512]{1,0:T(8,128)(2,1)S(1)}, bf16[64,512]{1,0:T(8,128)(2,1)S(1)}, u32[]{:S(2)}, u32[]{:S(2)}) collective-permute-start(bf16[64,512]{1,0:T(8,128)(2,1)S(1)} %bitcast.38), channel_id=1, source_target_pairs={{0,1},{1,0},{2,3},{3,2},{4,5},{5,4},{6,7},{7,6},{8,9},{9,8},{10,11... | collective-permute-start | bytes 196616 | tf_op jit(solution)/shard_map/ppermute | solution.py:147
  10.9 17.0 %copy-start.7 = (s32[16]{0:T(128)S(1)}, s32[16]{0:T(128)}, u32[]{:S(2)}) copy-start(s32[16]{0:T(128)} %param.12) | copy-start | bytes 196
  17.3 29.0 %copy-start.8 = (s32[16]{0:T(128)S(1)}, s32[16]{0:T(128)}, u32[]{:S(2)}) copy-start(s32[16]{0:T(128)} %param.13) | copy-start | bytes 196
  20.6 26.0 %collective-permute-start.10 = (bf16[816,512]{1,0:T(8,128)(2,1)}, bf16[816,512]{1,0:T(8,128)(2,1)}, u32[]{:S(2)}, u32[]{:S(2)}) collective-permute-start(bf16[816,512]{1,0:T(8,128)(2,1)} %get-tuple-element.39), channel_id=1, source_target_pairs={{0,2},{1,3},{2,0},{3,1},{4,6},{5,7},{6,4},{7,5},{8,10},{9,11},{10,... | collective-permute-start | bytes 2506760 | tf_op jit(solution)/shard_map/ppermute | solution.py:147
  23.5 10.7 %collective-permute-start.3 = (bf16[400,256]{1,0:T(8,128)(2,1)}, bf16[400,256]{1,0:T(8,128)(2,1)S(1)}, u32[]{:S(2)}, u32[]{:S(2)}) collective-permute-start(bf16[400,256]{1,0:T(8,128)(2,1)} %get-tuple-element.33), channel_id=1, source_target_pairs={{0,4},{1,5},{2,6},{3,7},{4,0},{5,1},{6,2},{7,3},{8,12},{9,13},{10,... | collective-permute-start | bytes 614408 | tf_op jit(solution)/shard_map/ppermute | solution.py:147
  25.1 17.9 %collective-permute-start.4 = (bf16[400,256]{1,0:T(8,128)(2,1)}, bf16[400,256]{1,0:T(8,128)(2,1)}, u32[]{:S(2)}, u32[]{:S(2)}) collective-permute-start(bf16[400,256]{1,0:T(8,128)(2,1)} %get-tuple-element.34), channel_id=1, source_target_pairs={{0,8},{1,9},{2,10},{3,11},{4,12},{5,13},{6,14},{7,15},{8,0},{9,1},... | collective-permute-start | bytes 614408 | tf_op jit(solution)/shard_map/ppermute | solution.py:147
  27.7 15.4 %collective-permute-start.5 = (bf16[400,256]{1,0:T(8,128)(2,1)}, bf16[400,256]{1,0:T(8,128)(2,1)}, u32[]{:S(2)}, u32[]{:S(2)}) collective-permute-start(bf16[400,256]{1,0:T(8,128)(2,1)} %get-tuple-element.35), channel_id=1, source_target_pairs={{0,12},{1,13},{2,14},{3,15},{4,8},{5,9},{6,10},{7,11},{8,4},{9,5},... | collective-permute-start | bytes 614408 | tf_op jit(solution)/shard_map/ppermute | solution.py:147
  34.2 0.7 copy-start.5
  43.0 0.9 copy-start.6
  45.9 8.8 %collective-permute-start.6 = (bf16[1296,128]{1,0:T(8,128)(2,1)}, bf16[1296,128]{1,0:T(8,128)(2,1)S(1)}, u32[]{:S(2)}, u32[]{:S(2)}) collective-permute-start(bf16[1296,128]{1,0:T(8,128)(2,1)} %get-tuple-element.36), channel_id=1, source_target_pairs={{0,2},{1,3},{2,0},{3,1},{4,6},{5,7},{6,4},{7,5},{8,10},{9,11},{10,... | collective-permute-start | bytes 995336 | tf_op jit(solution)/shard_map/ppermute | solution.py:147
  48.5 10.1 %collective-permute-start.11 = (bf16[816,128]{1,0:T(8,128)(2,1)S(1)}, bf16[816,128]{1,0:T(8,128)(2,1)S(1)}, u32[]{:S(2)}, u32[]{:S(2)}) collective-permute-start(bf16[816,128]{1,0:T(8,128)(2,1)S(1)} %get-tuple-element.41), channel_id=1, source_target_pairs={{0,4},{1,5},{2,6},{3,7},{4,0},{5,1},{6,2},{7,3},{8,12},{9,13},{10,... | collective-permute-start | bytes 626696 | tf_op jit(solution)/shard_map/ppermute | solution.py:147
  52.1 17.5 %collective-permute-start.12 = (bf16[816,128]{1,0:T(8,128)(2,1)}, bf16[816,128]{1,0:T(8,128)(2,1)S(1)}, u32[]{:S(2)}, u32[]{:S(2)}) collective-permute-start(bf16[816,128]{1,0:T(8,128)(2,1)} %get-tuple-element.42), channel_id=1, source_target_pairs={{0,8},{1,9},{2,10},{3,11},{4,12},{5,13},{6,14},{7,15},{8,0},{9,1},... | collective-permute-start | bytes 626696 | tf_op jit(solution)/shard_map/ppermute | solution.py:147
  53.1 16.5 %collective-permute-start.13 = (bf16[816,128]{1,0:T(8,128)(2,1)S(1)}, bf16[816,128]{1,0:T(8,128)(2,1)S(1)}, u32[]{:S(2)}, u32[]{:S(2)}) collective-permute-start(bf16[816,128]{1,0:T(8,128)(2,1)S(1)} %get-tuple-element.43), channel_id=1, source_target_pairs={{0,12},{1,13},{2,14},{3,15},{4,8},{5,9},{6,10},{7,11},{8,4},{9,5},... | collective-permute-start | bytes 626696 | tf_op jit(solution)/shard_map/ppermute | solution.py:147
  54.6 15.4 %collective-permute-start.8 = (bf16[1024,128]{1,0:T(8,128)(2,1)S(1)}, bf16[1024,128]{1,0:T(8,128)(2,1)S(1)}, u32[]{:S(2)}, u32[]{:S(2)}) collective-permute-start(bf16[1024,128]{1,0:T(8,128)(2,1)S(1)} %get-tuple-element.37.so), channel_id=1, source_target_pairs={{0,1},{1,0},{2,3},{3,2},{4,5},{5,4},{6,7},{7,6},{8,9},{9,8},{10,11... | collective-permute-start | bytes 786440 | tf_op jit(solution)/shard_map/ppermute | solution.py:147
  58.6 16.7 %collective-permute-start.7 = (bf16[1296,128]{1,0:T(8,128)(2,1)S(1)}, bf16[1296,128]{1,0:T(8,128)(2,1)S(1)}, u32[]{:S(2)}, u32[]{:S(2)}) collective-permute-start(bf16[1296,128]{1,0:T(8,128)(2,1)S(1)} %collective-permute-done.6.so.b1), channel_id=1, source_target_pairs={{0,1},{1,0},{2,3},{3,2},{4,5},{5,4},{6,7},{7,6},{8,9},{9,8},{10,11... | collective-permute-start | bytes 995336 | tf_op jit(solution)/shard_map/ppermute | solution.py:147
  69.9 12.3 %collective-permute-start.14 = (bf16[1152,128]{1,0:T(8,128)(2,1)S(1)}, bf16[1152,128]{1,0:T(8,128)(2,1)S(1)}, u32[]{:S(2)}, u32[]{:S(2)}) collective-permute-start(bf16[1152,128]{1,0:T(8,128)(2,1)S(1)} %shard_map.82.kv0), channel_id=1, source_target_pairs={{0,1},{1,0},{2,3},{3,2},{4,5},{5,4},{6,7},{7,6},{8,9},{9,8},{10,11... | collective-permute-start | bytes 884744 | tf_op jit(solution)/shard_map/ppermute | solution.py:147
  70.0 3.4 %copy-start.1 = (bf16[8192,512]{1,0:T(8,128)(2,1)S(1)}, bf16[8192,512]{1,0:T(8,128)(2,1)}, u32[]{:S(2)}) copy-start(bf16[8192,512]{1,0:T(8,128)(2,1)} %w_ref.8) | copy-start | bytes 25165828
  73.4 8.8 %slice-start = ((s8[8388608]{0:T(1024)(128)(4,1)}), s8[4194304]{0:T(1024)(128)(4,1)S(1)}, s32[]{:S(2)}) async-start(s8[8388608]{0:T(1024)(128)(4,1)} %bitcast.36), calls=%async_computation | async-start | bytes 8388608
  75.3 6.9 %slice-start.1 = ((s8[8388608]{0:T(1024)(128)(4,1)}), s8[4194304]{0:T(1024)(128)(4,1)S(1)}, s32[]{:S(2)}) async-start(s8[8388608]{0:T(1024)(128)(4,1)} %bitcast.36), calls=%async_computation.1 | async-start | bytes 8388608
  75.3 3.5 %copy-start.2 = (bf16[8192,512]{1,0:T(8,128)(2,1)S(1)}, bf16[8192,512]{1,0:T(8,128)(2,1)}, u32[]{:S(2)}) copy-start(bf16[8192,512]{1,0:T(8,128)(2,1)} %w_ref.8) | copy-start | bytes 25165828
  80.8 1.5 %collective-permute-start.9 = (bf16[64,512]{1,0:T(8,128)(2,1)S(1)}, bf16[64,512]{1,0:T(8,128)(2,1)S(1)}, u32[]{:S(2)}, u32[]{:S(2)}) collective-permute-start(bf16[64,512]{1,0:T(8,128)(2,1)S(1)} %shard_map.80.q0), channel_id=1, source_target_pairs={{0,1},{1,0},{2,3},{3,2},{4,5},{5,4},{6,7},{7,6},{8,9},{9,8},{10,11... | collective-permute-start | bytes 196616 | tf_op jit(solution)/shard_map/ppermute | solution.py:147
  88.9 9.2 %collective-permute-start.20 = (bf16[64,512]{1,0:T(8,128)(2,1)S(1)}, bf16[64,512]{1,0:T(8,128)(2,1)S(1)}, u32[]{:S(2)}, u32[]{:S(2)}) collective-permute-start(bf16[64,512]{1,0:T(8,128)(2,1)S(1)} %get-tuple-element.52), channel_id=1, source_target_pairs={{0,6},{1,7},{2,4},{3,5},{4,2},{5,3},{6,0},{7,1},{8,14},{9,15},{10,... | collective-permute-start | bytes 196616 | tf_op jit(solution)/shard_map/ppermute | solution.py:147
  92.8 6.8 %collective-permute-start.21 = (bf16[64,512]{1,0:T(8,128)(2,1)S(1)}, bf16[64,512]{1,0:T(8,128)(2,1)S(1)}, u32[]{:S(2)}, u32[]{:S(2)}) collective-permute-start(bf16[64,512]{1,0:T(8,128)(2,1)S(1)} %get-tuple-element.53), channel_id=1, source_target_pairs={{0,4},{1,5},{2,6},{3,7},{4,0},{5,1},{6,2},{7,3},{8,12},{9,13},{10,... | collective-permute-start | bytes 196616 | tf_op jit(solution)/shard_map/ppermute | solution.py:147
  92.8 8.3 %collective-permute-start.22 = (bf16[64,512]{1,0:T(8,128)(2,1)S(1)}, bf16[64,512]{1,0:T(8,128)(2,1)S(1)}, u32[]{:S(2)}, u32[]{:S(2)}) collective-permute-start(bf16[64,512]{1,0:T(8,128)(2,1)S(1)} %get-tuple-element.54), channel_id=1, source_target_pairs={{0,2},{1,3},{2,0},{3,1},{4,6},{5,7},{6,4},{7,5},{8,10},{9,11},{10,... | collective-permute-start | bytes 196616 | tf_op jit(solution)/shard_map/ppermute | solution.py:147
  93.4 7.7 %collective-permute-start.16 = (bf16[64,512]{1,0:T(8,128)(2,1)S(1)}, bf16[64,512]{1,0:T(8,128)(2,1)S(1)}, u32[]{:S(2)}, u32[]{:S(2)}) collective-permute-start(bf16[64,512]{1,0:T(8,128)(2,1)S(1)} %get-tuple-element.48), channel_id=1, source_target_pairs={{0,14},{1,15},{2,12},{3,13},{4,10},{5,11},{6,8},{7,9},{8,6},{9,7},... | collective-permute-start | bytes 196616 | tf_op jit(solution)/shard_map/ppermute | solution.py:147
  96.7 6.1 %collective-permute-start.17 = (bf16[64,512]{1,0:T(8,128)(2,1)S(1)}, bf16[64,512]{1,0:T(8,128)(2,1)S(1)}, u32[]{:S(2)}, u32[]{:S(2)}) collective-permute-start(bf16[64,512]{1,0:T(8,128)(2,1)S(1)} %get-tuple-element.49), channel_id=1, source_target_pairs={{0,12},{1,13},{2,14},{3,15},{4,8},{5,9},{6,10},{7,11},{8,4},{9,5},... | collective-permute-start | bytes 196616 | tf_op jit(solution)/shard_map/ppermute | solution.py:147
  98.1 10.5 %collective-permute-start.18 = (bf16[64,512]{1,0:T(8,128)(2,1)S(1)}, bf16[64,512]{1,0:T(8,128)(2,1)S(1)}, u32[]{:S(2)}, u32[]{:S(2)}) collective-permute-start(bf16[64,512]{1,0:T(8,128)(2,1)S(1)} %get-tuple-element.50), channel_id=1, source_target_pairs={{0,10},{1,11},{2,8},{3,9},{4,14},{5,15},{6,12},{7,13},{8,2},{9,3},... | collective-permute-start | bytes 196616 | tf_op jit(solution)/shard_map/ppermute | solution.py:147
  99.6 9.7 %collective-permute-start.19 = (bf16[64,512]{1,0:T(8,128)(2,1)S(1)}, bf16[64,512]{1,0:T(8,128)(2,1)S(1)}, u32[]{:S(2)}, u32[]{:S(2)}) collective-permute-start(bf16[64,512]{1,0:T(8,128)(2,1)S(1)} %get-tuple-element.51), channel_id=1, source_target_pairs={{0,8},{1,9},{2,10},{3,11},{4,12},{5,13},{6,14},{7,15},{8,0},{9,1},... | collective-permute-start | bytes 196616 | tf_op jit(solution)/shard_map/ppermute | solution.py:147
